TPU v7x, 32 devices: a whole 2x2x4 slice. The times are simulated.
32 devices in a mesh: seq: 4 (over x, core), exp: 8 (over z, y).
Axes of the slice: x: 2, y: 2, z: 4, core: 2. Of those that a mesh axis runs over, the one named last changes fastest.
Arguments:
- residual_in: bfloat16 [4096, 2048], P(('seq', 'exp')), may hold values from -8 to 8
- ssm_input: bfloat16 [4096, 2048], P(('seq', 'exp')), may hold values from -6 to 6
- ssm_b: bfloat16 [4096, 128], P(('seq', 'exp')), may hold values from -6 to 6
- ssm_c: bfloat16 [4096, 128], P(('seq', 'exp')), may hold values from -0.5 to 0.5
- log_decay: float32 [4096, 32], P(('seq', 'exp')), may hold values from -2 to 0, as said below
- skip_gain: float32 [32], replicated, may hold values from 0.5 to 1.5
- out_proj: bfloat16 [2048, 2048], replicated, may hold values from -0.125 to 0.125
- norm_gain: float32 [2048], replicated, may hold values from 0.5 to 1.5
- router: bfloat16 [2048, 16], replicated, may hold values from -1 to 1
- assignment: int32 [4096, 1], P(('seq', 'exp')), may hold values from 0 to 15; in each aligned block of 128 rows (0 to 127, 128 to 255, ...) at most 16 rows name the same one
- expert_gate: bfloat16 [32, 2048, 704], P(('seq', 'exp')), may hold values from -0.125 to 0.125
- expert_up: bfloat16 [32, 2048, 704], P(('seq', 'exp')), may hold values from -0.125 to 0.125
- expert_down: bfloat16 [32, 704, 2048], P(('seq', 'exp')), may hold values from -0.15625 to 0.15625
Outputs:
- layer_out: bfloat16 [4096, 2048], P(('seq', 'exp'))
- route_weight: float32 [4096], P(('seq', 'exp'))
Inputs may be any that keep to these rules, and one draw needn't show every extreme that they name: `log_decay`: every entry is negative. `assignment`: on the rows of one device no expert is named more than 16 times; in every draw some expert is named exactly 16 times on some device.
All inputs are finite; a program needn't handle non-finite values.
Results may differ from a plain program's by a relative error of at most 0.009.
Values may be sent and summed in bfloat16 or wider, within the bound.
A program may use at most 576 MiB of HBM per device.

v0:
```python
import jax
import jax.numpy as jnp
from jax import lax
from jax.sharding import PartitionSpec as P

BLOCK = 128
SINK_ITERS = 8


def entering(x, axis, combine, identity):
    devices, here = (lax.axis_size(axis), lax.axis_index(axis))
    everything = jax.tree.map(lambda part: lax.all_gather(part, axis), x)
    start = jax.tree.map(
        lambda part, zero: jnp.broadcast_to(jnp.asarray(zero, part.dtype), part.shape), x, identity
    )

    def turn(k, before):
        reached = k < here
        new = combine(before, jax.tree.map(lambda part: part[k], everything))
        return jax.tree.map(lambda a, b: jnp.where(reached, a, b), new, before)

    return lax.fori_loop(0, devices, turn, start)


def widen(per_head, width):
    return jnp.repeat(per_head, width // per_head.shape[-1], axis=-1)


def block_terms(values, b_blocks, c_blocks, decay):
    block_count, length, head_count, head_size = values.shape
    cumulative = jnp.cumsum(decay, axis=1)
    weight = jnp.sqrt(-jnp.expm1(2.0 * decay))
    scores = jnp.einsum("ktn,ksn->kts", c_blocks, b_blocks, preferred_element_type=jnp.float32)
    leading = jnp.swapaxes(cumulative, 1, 2)
    distance = leading[:, :, :, None] - leading[:, :, None, :]
    causal = jnp.arange(length)[:, None] >= jnp.arange(length)[None, :]
    decay_mix = jnp.where(causal, jnp.exp(jnp.minimum(distance, 0.0)), 0.0) * (
        jnp.swapaxes(weight, 1, 2)[:, :, None, :] * scores[:, None, :, :]
    )
    decay_mix = decay_mix.astype(jnp.bfloat16)
    inner_part = jnp.einsum(
        "khts,kshp->kthp", decay_mix, values, preferred_element_type=jnp.float32
    )
    inner_part = inner_part.reshape(block_count, length, head_count * head_size)
    tail_weight = jnp.exp(cumulative[:, -1:, :] - cumulative) * weight
    row_width = head_count * head_size
    flat_values = values.reshape(block_count, length, row_width)
    tail_in = (flat_values.astype(jnp.float32) * widen(tail_weight, row_width)).astype(jnp.bfloat16)
    block_state = jnp.einsum("ksn,ksc->knc", b_blocks, tail_in, preferred_element_type=jnp.float32)
    return (inner_part, cumulative, block_state)


def combine_states(earlier, following):
    factor = widen(jnp.exp(following[0]), earlier[1].shape[1])
    return (earlier[0] + following[0], factor[None, :] * earlier[1] + following[1])


def local_step(entry, pieces):
    total, state = pieces
    return (widen(jnp.exp(total), entry.shape[1])[None, :] * entry + state, entry)


def balance(kernel, chosen_hot):
    column = jnp.ones((kernel.shape[1],), jnp.float32)
    for sweep in range(SINK_ITERS):
        row_scale = 1.0 / jnp.sum(kernel * column[None, :], axis=1)
        column = 1.0 / lax.psum(jnp.sum(kernel * row_scale[:, None], axis=0), ("seq", "exp"))
    weighted = kernel * column[None, :]
    return (
        kernel.shape[1]
        * jnp.sum(jnp.where(chosen_hot, weighted, 0.0), axis=1)
        / jnp.sum(weighted, axis=1)
    )


def feed_forward(arrived, gate_full, up_full, down_full):
    sources, slots, model_width = arrived.shape
    flat = arrived.reshape(sources * slots, model_width)
    gate_val = jnp.dot(flat, gate_full, preferred_element_type=jnp.float32)
    up_val = jnp.dot(flat, up_full, preferred_element_type=jnp.float32)
    hidden = (jax.nn.silu(gate_val) * up_val).astype(jnp.bfloat16)
    return jnp.dot(hidden, down_full, preferred_element_type=jnp.float32).reshape(
        sources, slots, model_width
    )


def per_device(
    residual_in,
    ssm_input,
    ssm_b,
    ssm_c,
    log_decay,
    skip_gain,
    out_proj,
    norm_gain,
    router,
    assignment,
    expert_gate,
    expert_up,
    expert_down,
):
    head_count = skip_gain.shape[0]
    length, row_width = ssm_input.shape
    head_size = row_width // head_count
    state_size = ssm_b.shape[1]
    model_width = residual_in.shape[1]
    block_count = length // BLOCK
    values = ssm_input.reshape(block_count, BLOCK, head_count, head_size)
    b_blocks = ssm_b.reshape(block_count, BLOCK, state_size)
    c_blocks = ssm_c.reshape(block_count, BLOCK, state_size)
    decay = log_decay.reshape(block_count, BLOCK, head_count)
    inner_part, cumulative, block_state = block_terms(values, b_blocks, c_blocks, decay)
    block_total = cumulative[:, -1, :]
    device_state, local_entry = lax.scan(
        local_step, jnp.zeros_like(block_state[0]), (block_total, block_state)
    )
    prefix_log = jnp.cumsum(block_total, axis=0) - block_total
    device_log = jnp.sum(block_total, axis=0)
    identity = (jnp.zeros((head_count,), jnp.float32), jnp.zeros_like(device_state))
    earlier_log, carried_in = entering(
        (device_log, device_state), ("seq", "exp"), combine_states, identity
    )
    entry = widen(jnp.exp(prefix_log), row_width)[:, None, :] * carried_in[None] + local_entry
    entry_rounded = entry.astype(jnp.bfloat16)
    carried = widen(jnp.exp(cumulative), row_width) * jnp.einsum(
        "ktn,knc->ktc", c_blocks, entry_rounded, preferred_element_type=jnp.float32
    )
    skip_wide = widen(skip_gain, row_width)
    flat_values = ssm_input.reshape(block_count, BLOCK, row_width).astype(jnp.float32)
    scan_out = (
        (inner_part + carried + skip_wide[None, None, :] * flat_values)
        .reshape(length, row_width)
        .astype(jnp.bfloat16)
    )
    mixed = residual_in.astype(jnp.float32) + jnp.dot(
        scan_out, out_proj, preferred_element_type=jnp.float32
    )
    scale = lax.rsqrt(jnp.mean(mixed * mixed, axis=1, keepdims=True) + 1e-05)
    normed = (mixed * scale * norm_gain[None, :]).astype(jnp.bfloat16)
    kernel = jnp.exp(jnp.dot(normed, router, preferred_element_type=jnp.float32))
    experts = router.shape[1]
    capacity = 2 * length // experts
    chosen = assignment[:, 0]
    chosen_hot = chosen[:, None] == jnp.arange(experts, dtype=jnp.int32)[None, :]
    route_weight = balance(kernel, chosen_hot)
    hot_int = chosen_hot.astype(jnp.int32)
    slot = jnp.sum(jnp.cumsum(hot_int, axis=0) * hot_int, axis=1) - 1
    position = chosen * capacity + slot
    packed = jnp.zeros((experts * capacity, model_width), jnp.bfloat16).at[position].set(normed)
    doubled = jnp.broadcast_to(
        packed.reshape(experts, 1, capacity, model_width), (experts, 2, capacity, model_width)
    )
    doubled = doubled.reshape(2 * experts, capacity, model_width)
    partial_value = feed_forward(
        lax.all_to_all(doubled, ("seq", "exp"), split_axis=0, concat_axis=0, tiled=True),
        expert_gate[0],
        expert_up[0],
        expert_down[0],
    )
    returned = lax.all_to_all(
        partial_value.astype(jnp.bfloat16), ("seq", "exp"), split_axis=0, concat_axis=0, tiled=True
    ).astype(partial_value.dtype)
    summed = jnp.sum(returned.reshape(experts, 2, capacity, model_width), axis=1).astype(
        jnp.bfloat16
    )
    summed = summed.reshape(experts * capacity, model_width)
    expert_out = summed[position]
    layer_out = (mixed + route_weight[:, None] * expert_out.astype(jnp.float32)).astype(
        jnp.bfloat16
    )
    return (layer_out, route_weight)


def solution(mesh):
    in_specs = (
        P(("seq", "exp"), None),
        P(("seq", "exp"), None),
        P(("seq", "exp"), None),
        P(("seq", "exp"), None),
        P(("seq", "exp"), None),
        P(),
        P(),
        P(),
        P(),
        P(("seq", "exp"), None),
        P(("seq", "exp"), None, None),
        P(("seq", "exp"), None, None),
        P(("seq", "exp"), None, None),
    )
    out_specs = (P(("seq", "exp"), None), P(("seq", "exp")))
    return jax.shard_map(
        per_device, mesh=mesh, in_specs=in_specs, out_specs=out_specs, check_vma=False
    )
```

profile of v0, /device:TPU:0, one launch (start us, length us, event | category | flops | bytes accessed | tf_op | source)
XLA Modules:
  0.0 762.2 jit_solution(15610699507661942850)
XLA Ops:
  19.5 69.7 %all-gather = f32[32,1,32]{2,1,0:T(1,128)S(1)} all-gather(f32[1,1,32]{2,1,0:T(1,128)} %get-tuple-element.165), channel_id=2, replica_groups=mesh['seq'=4,'exp'=8] {'seq','exp'}, dimensions={0}, use_global_device_ids=true | all-gather | bytes 4224 | tf_op jit(solution)/shard_map/all_gather | solution.py:12
  94.2 108.1 %all-gather.4.cloned.1.call-done = f32[4096,2048]{0,1:T(8,128)} async-done(((f32[128,2048]{0,1:T(8,128)}), f32[4096,2048]{0,1:T(8,128)}) %all-gather.4.cloned.1.call-update) | async-done | bytes 33554448 | tf_op jit(solution)/shard_map/all_gather | solution.py:12
  202.3 33.4 %copy.62 = f32[4096,2048]{1,0:T(8,128)} copy(f32[4096,2048]{0,1:T(8,128)} %all-gather.4.cloned.1.call-done) | data formatting | bytes 67108864
  235.7 92.5 %while.9 = (s32[]{:T(128)}, f32[128,2048]{1,0:T(8,128)}, s32[]{:T(128)}, f32[32,32]{1,0:T(8,128)S(1)}, f32[32,128,2048]{2,1,0:T(8,128)}, /*index=5*/s32[]{:T(128)}, s32[]{:T(128)}) while((s32[]{:T(128)}, f32[128,2048]{1,0:T(8,128)}, s32[]{:T(128)}, f32[32,32]{1,0:T(8,128)S(1)}, f32[32,128,2048]{2,1,0:T(8,128)}, ...), condition=%wide.region_2.3_spmd.clone, body=%wide.region_1.2_spmd.clone.sunk | while | flops 1048580 | bytes 3178985 | solution.py:22
  238.5 2.7 fusion.50
  241.4 2.7 fusion.50
  244.3 2.7 fusion.50
  247.2 2.7 fusion.50
  250.1 2.7 fusion.50
  253.0 2.7 fusion.50
  255.9 2.7 fusion.50
  258.8 2.7 fusion.50
  261.7 2.7 fusion.50
  264.6 2.7 fusion.50
  267.5 2.7 fusion.50
  270.4 2.7 fusion.50
  273.3 2.7 fusion.50
  276.2 2.7 fusion.50
  279.1 2.7 fusion.50
  282.0 2.7 fusion.50
  284.9 2.7 fusion.50
  287.8 2.7 fusion.50
  290.7 2.7 fusion.50
  293.6 2.7 fusion.50
  296.5 2.7 fusion.50
  299.4 2.7 fusion.50
  308.1 2.7 fusion.50
  316.8 2.7 fusion.50
  319.7 2.7 fusion.50
  325.5 2.7 fusion.50
  329.3 7.1 multiply_reduce_fusion
  336.4 3.2 scatter_custom_fusion
  339.7 2.8 broadcast_in_dim.94
  342.4 6.6 all-to-all-start
  350.8 67.1 %psum.56 = f32[16]{0:T(128)S(1)} all-reduce(f32[16]{0:T(128)S(1)} %multiply_reduce_fusion.15), channel_id=1, replica_groups=mesh['seq'=4,'exp'=8] {'seq','exp'}, use_global_device_ids=true, to_apply=%region_6.7 | all-reduce | flops 16 | bytes 128 | tf_op jit(solution)/shard_map/psum | solution.py:67
  418.2 38.7 %psum.57 = f32[16]{0:T(128)S(1)} all-reduce(f32[16]{0:T(128)S(1)} %multiply_reduce_fusion.13), channel_id=1, replica_groups=mesh['seq'=4,'exp'=8] {'seq','exp'}, use_global_device_ids=true, to_apply=%region_9.10 | all-reduce | flops 16 | bytes 128 | tf_op jit(solution)/shard_map/psum | solution.py:67
  457.0 4.3 fusion.4
  461.3 4.3 fusion.14
  467.9 4.2 convolution_convert_fusion
  472.1 6.0 all-to-all-start.1
  478.2 68.7 %psum.58 = f32[16]{0:T(128)S(1)} all-reduce(f32[16]{0:T(128)S(1)} %multiply_reduce_fusion.11), channel_id=1, replica_groups=mesh['seq'=4,'exp'=8] {'seq','exp'}, use_global_device_ids=true, to_apply=%region_12.13 | all-reduce | flops 16 | bytes 128 | tf_op jit(solution)/shard_map/psum | solution.py:67
  547.2 38.5 %psum.59 = f32[16]{0:T(128)S(1)} all-reduce(f32[16]{0:T(128)S(1)} %multiply_reduce_fusion.9), channel_id=1, replica_groups=mesh['seq'=4,'exp'=8] {'seq','exp'}, use_global_device_ids=true, to_apply=%region_15.16 | all-reduce | flops 16 | bytes 128 | tf_op jit(solution)/shard_map/psum | solution.py:67
  585.9 41.5 %psum.60 = f32[16]{0:T(128)S(1)} all-reduce(f32[16]{0:T(128)S(1)} %multiply_reduce_fusion.7), channel_id=1, replica_groups=mesh['seq'=4,'exp'=8] {'seq','exp'}, use_global_device_ids=true, to_apply=%region_18.19 | all-reduce | flops 16 | bytes 128 | tf_op jit(solution)/shard_map/psum | solution.py:67
  627.7 38.5 %psum.61 = f32[16]{0:T(128)S(1)} all-reduce(f32[16]{0:T(128)S(1)} %multiply_reduce_fusion.5), channel_id=1, replica_groups=mesh['seq'=4,'exp'=8] {'seq','exp'}, use_global_device_ids=true, to_apply=%region_21.22 | all-reduce | flops 16 | bytes 128 | tf_op jit(solution)/shard_map/psum | solution.py:67
  666.4 41.5 %psum.62 = f32[16]{0:T(128)S(1)} all-reduce(f32[16]{0:T(128)S(1)} %multiply_reduce_fusion.3), channel_id=1, replica_groups=mesh['seq'=4,'exp'=8] {'seq','exp'}, use_global_device_ids=true, to_apply=%region_24.25 | all-reduce | flops 16 | bytes 128 | tf_op jit(solution)/shard_map/psum | solution.py:67
  708.2 38.7 %psum.63 = f32[16]{0:T(128)S(1)} all-reduce(f32[16]{0:T(128)S(1)} %multiply_reduce_fusion.1), channel_id=1, replica_groups=mesh['seq'=4,'exp'=8] {'seq','exp'}, use_global_device_ids=true, to_apply=%region_27.28 | all-reduce | flops 16 | bytes 128 | tf_op jit(solution)/shard_map/psum | solution.py:67
  747.0 3.3 bitcast_reduce_fusion
  750.4 2.8 gather_fusion
  (191 shorter events, 47.2 us)
Async XLA Ops:
  7.2 460.7 %copy-start = (bf16[1,704,2048]{2,1,0:T(8,128)(2,1)S(1)}, bf16[1,704,2048]{2,1,0:T(8,128)(2,1)}, u32[]{:S(2)}) copy-start(bf16[1,704,2048]{2,1,0:T(8,128)(2,1)} %param.27) | copy-start | bytes 8650756
  7.2 5.9 copy-start.2
  7.2 195.2 %all-gather.4.cloned.1.call-start = ((), (), s32[]{:S(2)}) async-start(), calls=%async_computation.2 | async-start | bytes 34603008 | tf_op jit(solution)/shard_map/all_gather | solution.py:12
  235.7 93.6 %copy-start.1 = (bf16[128,128]{1,0:T(8,128)(2,1)S(1)}, bf16[128,128]{1,0:T(8,128)(2,1)}, u32[]{:S(2)}) copy-start(bf16[128,128]{1,0:T(8,128)(2,1)} %param.18) | copy-start | bytes 98308
  235.7 93.6 %copy-start.5 = (f32[2048]{0:T(1024)S(1)}, f32[2048]{0:T(1024)}, u32[]{:S(2)}) copy-start(f32[2048]{0:T(1024)} %broadcast_in_dim.48) | copy-start | bytes 24580
  235.7 93.6 %copy-start.6 = (f32[2048]{0:T(1024)S(1)}, f32[2048]{0:T(1024)}, u32[]{:S(2)}) copy-start(f32[2048]{0:T(1024)} %mul.305) | copy-start | bytes 24580
  329.3 7.1 copy-start.4
  342.4 6.7 copy-start.3
  342.4 114.5 %all-to-all-start = ((bf16[32,16,2048]{2,1,0:T(8,128)(2,1)}), bf16[32,16,2048]{2,1,0:T(8,128)(2,1)}, u32[]{:S(2)}, u32[]{:S(2)}) async-start(bf16[32,16,2048]{2,1,0:T(8,128)(2,1)} %bitcast.101), calls=%async_computation | async-start | bytes 4194304 | tf_op jit(solution)/shard_map/all_to_all | solution.py:155
  457.0 4.3 copy-start.9
  472.1 274.8 %copy-start.7 = (s32[128,1]{0,1:T(1,128)S(1)}, s32[128,1]{0,1:T(1,128)}, u32[]{:S(2)}) copy-start(s32[128,1]{0,1:T(1,128)} %param.24) | copy-start | bytes 1540
  472.1 274.9 %all-to-all-start.1 = ((bf16[32,16,2048]{2,1,0:T(8,128)(2,1)}), bf16[32,16,2048]{2,1,0:T(8,128)(2,1)}, u32[]{:S(2)}, u32[]{:S(2)}) async-start(bf16[32,16,2048]{2,1,0:T(8,128)(2,1)} %convolution_convert_fusion), calls=%async_computation.1 | async-start | bytes 4194304 | tf_op jit(solution)/shard_map/all_to_all | solution.py:160
  747.0 6.2 copy-start.8
Sparse Core Ops, SparseCore 0:
  15.2 187.0 all-gather.3
where the time goes:
time: 765 us; the launch traced here: 762 us
  blocking collectives  443 us (58%)
  waiting for transfers between devices  108 us (14%)
  other arithmetic  102 us (13%)
  local copies, waits for them, and re-layouts  54.4 us (7%)
  matrix products  27.2 us (4%)
  between operations  14.3 us (2%)
  starting transfers between devices  12.7 us (2%)
    psum x8, blocking collectives, balance(): lax.psum(jnp.sum(kernel * row_scale[:, None], axis=0), ('seq', 'exp'))  373 us
    all_gather x1, waiting for transfers between devices, entering(): everything = jax.tree.map(lambda part: lax.all_gather(part, axis), x)  108 us
    select_n x32, other arithmetic, turn(): return jax.tree.map(lambda a, b: jnp.where(reached, a, b), new, before)  87.5 us
    all_gather x1, blocking collectives, entering(): everything = jax.tree.map(lambda part: lax.all_gather(part, axis), x)  69.7 us
    unnamed x22, local copies, waits for them, and re-layouts  34.7 us
  transfers between devices with their start and end apart: 3, of which 1 were waited for; matrix products, arithmetic and copies ran while one was open for 2% of the time, Pallas kernels for 0%

commit v1 on v0

--- a/solution.py
+++ b/solution.py
@@ -64,7 +64,9 @@
     column = jnp.ones((kernel.shape[1],), jnp.float32)
     for sweep in range(SINK_ITERS):
         row_scale = 1.0 / jnp.sum(kernel * column[None, :], axis=1)
-        column = 1.0 / lax.psum(jnp.sum(kernel * row_scale[:, None], axis=0), ("seq", "exp"))
+        column = 1.0 / lax.psum(
+            lax.psum(jnp.sum(kernel * row_scale[:, None], axis=0), "exp"), "seq"
+        )
     weighted = kernel * column[None, :]
     return (
         kernel.shape[1]

time: 765 us -> 658 us (0.86)
  blocking collectives: 443 us -> 339 us
    psum x8 -> x16, blocking collectives: 373 us -> 269 us  [the longest x8 224 us: balance(): lax.psum(jnp.sum(kernel * row_scale[:, None], axis=0), 'exp')]
where the time goes in v1:
time: 658 us; the launch traced here: 656 us
  blocking collectives  339 us (52%)
  waiting for transfers between devices  108 us (16%)
  other arithmetic  102 us (16%)
  local copies, waits for them, and re-layouts  54.4 us (8%)
  matrix products  27.2 us (4%)
  between operations  14.3 us (2%)
  starting transfers between devices  10.3 us (2%)
    psum x8, blocking collectives, balance(): lax.psum(jnp.sum(kernel * row_scale[:, None], axis=0), 'exp')  224 us
    all_gather x1, waiting for transfers between devices, entering(): everything = jax.tree.map(lambda part: lax.all_gather(part, axis), x)  108 us
    select_n x32, other arithmetic, turn(): return jax.tree.map(lambda a, b: jnp.where(reached, a, b), new, before)  87.5 us
    all_gather x1, blocking collectives, entering(): everything = jax.tree.map(lambda part: lax.all_gather(part, axis), x)  69.7 us
    psum x8, blocking collectives, balance(): lax.psum(lax.psum(jnp.sum(kernel * row_scale[:, None], axis=0), 'exp'), '...  45.4 us
    unnamed x22, local copies, waits for them, and re-layouts  34.7 us
  transfers between devices with their start and end apart: 3, of which 1 were waited for; matrix products, arithmetic and copies ran while one was open for 2% of the time, Pallas kernels for 0%

profile of v1, /device:TPU:0, one launch (start us, length us, event | category | flops | bytes accessed | tf_op | source)
XLA Modules:
  0.0 655.6 jit_solution(3492578408763274275)
XLA Ops:
  19.5 69.7 %all-gather = f32[32,1,32]{2,1,0:T(1,128)S(1)} all-gather(f32[1,1,32]{2,1,0:T(1,128)} %get-tuple-element.165), channel_id=2, replica_groups=mesh['seq'=4,'exp'=8] {'seq','exp'}, dimensions={0}, use_global_device_ids=true | all-gather | bytes 4224 | tf_op jit(solution)/shard_map/all_gather | solution.py:12
  94.2 108.1 %all-gather.4.cloned.1.call-done = f32[4096,2048]{0,1:T(8,128)} async-done(((f32[128,2048]{0,1:T(8,128)}), f32[4096,2048]{0,1:T(8,128)}) %all-gather.4.cloned.1.call-update) | async-done | bytes 33554448 | tf_op jit(solution)/shard_map/all_gather | solution.py:12
  202.3 33.4 %copy.62 = f32[4096,2048]{1,0:T(8,128)} copy(f32[4096,2048]{0,1:T(8,128)} %all-gather.4.cloned.1.call-done) | data formatting | bytes 67108864
  235.7 92.5 %while.9 = (s32[]{:T(128)}, f32[128,2048]{1,0:T(8,128)}, s32[]{:T(128)}, f32[32,32]{1,0:T(8,128)S(1)}, f32[32,128,2048]{2,1,0:T(8,128)}, /*index=5*/s32[]{:T(128)}, s32[]{:T(128)}) while((s32[]{:T(128)}, f32[128,2048]{1,0:T(8,128)}, s32[]{:T(128)}, f32[32,32]{1,0:T(8,128)S(1)}, f32[32,128,2048]{2,1,0:T(8,128)}, ...), condition=%wide.region_2.3_spmd.clone, body=%wide.region_1.2_spmd.clone.sunk | while | flops 1048580 | bytes 3178985 | solution.py:22
  238.5 2.7 fusion.50
  241.4 2.7 fusion.50
  244.3 2.7 fusion.50
  247.2 2.7 fusion.50
  253.0 2.7 fusion.50
  261.7 2.7 fusion.50
  264.6 2.7 fusion.50
  270.4 2.7 fusion.50
  273.3 2.7 fusion.50
  279.1 2.7 fusion.50
  282.0 2.7 fusion.50
  287.8 2.7 fusion.50
  290.7 2.7 fusion.50
  299.4 2.7 fusion.50
  308.1 2.7 fusion.50
  316.8 2.7 fusion.50
  319.7 2.7 fusion.50
  325.5 2.7 fusion.50
  329.3 7.1 %multiply_reduce_fusion = (f32[128]{0:T(128)S(1)}, f32[128,2048]{1,0:T(8,128)}) fusion(bf16[2048,2048]{1,0:T(8,128)(2,1)} %param.21, f32[128,2048]{0,1:T(8,128)} %bitcast.105, f32[128,2048]{0,1:T(8,128)} %bitcast.104, bf16[128,128]{1,0:T(8,128)(2,1)S(1)} %copy-done.1, bf16[128,2048]{0,1:T(8,128)(2,1)S(1)} %copy.55, f32[128,2048]{1,0:T(8,128)} %get-tuple-element.111, ...), kind=kOutput, calls=%fused_computation.30 | convolution fusion | flops 1143996288 | bytes 13681152 | tf_op jit(solution)/shard_map/dot_general | solution.py:137
  336.4 3.2 scatter_custom_fusion
  339.7 2.8 broadcast_in_dim.94
  342.4 6.6 %all-to-all-start = ((bf16[32,16,2048]{2,1,0:T(8,128)(2,1)}), bf16[32,16,2048]{2,1,0:T(8,128)(2,1)}, u32[]{:S(2)}, u32[]{:S(2)}) async-start(bf16[32,16,2048]{2,1,0:T(8,128)(2,1)} %bitcast.101), calls=%async_computation | async-start | bytes 4194304 | tf_op jit(solution)/shard_map/all_to_all | solution.py:157
  350.8 48.6 %psum.112 = f32[16]{0:T(128)S(1)} all-reduce(f32[16]{0:T(128)S(1)} %multiply_reduce_fusion.15), channel_id=1, replica_groups=mesh['seq'=4,'exp'=8] {'exp'}, use_global_device_ids=true, to_apply=%region_6.7 | all-reduce | flops 16 | bytes 128 | tf_op jit(solution)/shard_map/psum | solution.py:68
  399.4 5.6 psum.113
  405.3 26.2 %psum.114 = f32[16]{0:T(128)S(1)} all-reduce(f32[16]{0:T(128)S(1)} %multiply_reduce_fusion.13), channel_id=1, replica_groups=mesh['seq'=4,'exp'=8] {'exp'}, use_global_device_ids=true, to_apply=%region_10.11 | all-reduce | flops 16 | bytes 128 | tf_op jit(solution)/shard_map/psum | solution.py:68
  431.5 5.6 psum.115
  437.3 4.3 fusion.4
  441.6 4.3 fusion.14
  448.1 4.2 convolution_convert_fusion
  452.4 3.6 all-to-all-start.1
  456.1 49.8 %psum.116 = f32[16]{0:T(128)S(1)} all-reduce(f32[16]{0:T(128)S(1)} %multiply_reduce_fusion.11), channel_id=1, replica_groups=mesh['seq'=4,'exp'=8] {'exp'}, use_global_device_ids=true, to_apply=%region_14.15 | all-reduce | flops 16 | bytes 128 | tf_op jit(solution)/shard_map/psum | solution.py:68
  505.9 5.8 psum.117
  512.0 26.5 %psum.118 = f32[16]{0:T(128)S(1)} all-reduce(f32[16]{0:T(128)S(1)} %multiply_reduce_fusion.9), channel_id=1, replica_groups=mesh['seq'=4,'exp'=8] {'exp'}, use_global_device_ids=true, to_apply=%region_18.19 | all-reduce | flops 16 | bytes 128 | tf_op jit(solution)/shard_map/psum | solution.py:68
  538.4 5.6 psum.119
  544.3 17.2 %psum.120 = f32[16]{0:T(128)S(1)} all-reduce(f32[16]{0:T(128)S(1)} %multiply_reduce_fusion.7), channel_id=1, replica_groups=mesh['seq'=4,'exp'=8] {'exp'}, use_global_device_ids=true, to_apply=%region_22.23 | all-reduce | flops 16 | bytes 128 | tf_op jit(solution)/shard_map/psum | solution.py:68
  561.5 5.6 psum.121
  567.3 19.1 %psum.122 = f32[16]{0:T(128)S(1)} all-reduce(f32[16]{0:T(128)S(1)} %multiply_reduce_fusion.5), channel_id=1, replica_groups=mesh['seq'=4,'exp'=8] {'exp'}, use_global_device_ids=true, to_apply=%region_26.27 | all-reduce | flops 16 | bytes 128 | tf_op jit(solution)/shard_map/psum | solution.py:68
  586.5 5.6 psum.123
  592.4 17.1 %psum.124 = f32[16]{0:T(128)S(1)} all-reduce(f32[16]{0:T(128)S(1)} %multiply_reduce_fusion.3), channel_id=1, replica_groups=mesh['seq'=4,'exp'=8] {'exp'}, use_global_device_ids=true, to_apply=%region_30.31 | all-reduce | flops 16 | bytes 128 | tf_op jit(solution)/shard_map/psum | solution.py:68
  609.5 5.6 psum.125
  615.4 19.2 %psum.126 = f32[16]{0:T(128)S(1)} all-reduce(f32[16]{0:T(128)S(1)} %multiply_reduce_fusion.1), channel_id=1, replica_groups=mesh['seq'=4,'exp'=8] {'exp'}, use_global_device_ids=true, to_apply=%region_34.35 | all-reduce | flops 16 | bytes 128 | tf_op jit(solution)/shard_map/psum | solution.py:68
  634.6 5.6 psum.127
  640.3 3.3 bitcast_reduce_fusion
  643.7 2.8 gather_fusion
  (199 shorter events, 69.2 us)
Async XLA Ops:
  7.2 441.0 %copy-start = (bf16[1,704,2048]{2,1,0:T(8,128)(2,1)S(1)}, bf16[1,704,2048]{2,1,0:T(8,128)(2,1)}, u32[]{:S(2)}) copy-start(bf16[1,704,2048]{2,1,0:T(8,128)(2,1)} %param.27) | copy-start | bytes 8650756
  7.2 5.9 copy-start.2
  7.2 195.2 %all-gather.4.cloned.1.call-start = ((), (), s32[]{:S(2)}) async-start(), calls=%async_computation.2 | async-start | bytes 34603008 | tf_op jit(solution)/shard_map/all_gather | solution.py:12
  235.7 93.6 %copy-start.1 = (bf16[128,128]{1,0:T(8,128)(2,1)S(1)}, bf16[128,128]{1,0:T(8,128)(2,1)}, u32[]{:S(2)}) copy-start(bf16[128,128]{1,0:T(8,128)(2,1)} %param.18) | copy-start | bytes 98308
  235.7 93.6 %copy-start.5 = (f32[2048]{0:T(1024)S(1)}, f32[2048]{0:T(1024)}, u32[]{:S(2)}) copy-start(f32[2048]{0:T(1024)} %broadcast_in_dim.48) | copy-start | bytes 24580
  235.7 93.6 %copy-start.6 = (f32[2048]{0:T(1024)S(1)}, f32[2048]{0:T(1024)}, u32[]{:S(2)}) copy-start(f32[2048]{0:T(1024)} %mul.305) | copy-start | bytes 24580
  329.3 7.1 %copy-start.4 = (f32[2048]{0:T(1024)S(1)}, f32[2048]{0:T(1024)}, u32[]{:S(2)}) copy-start(f32[2048]{0:T(1024)} %param.22) | copy-start | bytes 24580
  342.4 6.7 %copy-start.3 = (bf16[2048,16]{0,1:T(8,128)(2,1)S(1)}, bf16[2048,16]{0,1:T(8,128)(2,1)}, u32[]{:S(2)}) copy-start(bf16[2048,16]{0,1:T(8,128)(2,1)} %param.23) | copy-start | bytes 196612
  342.4 94.8 %all-to-all-start = ((bf16[32,16,2048]{2,1,0:T(8,128)(2,1)}), bf16[32,16,2048]{2,1,0:T(8,128)(2,1)}, u32[]{:S(2)}, u32[]{:S(2)}) async-start(bf16[32,16,2048]{2,1,0:T(8,128)(2,1)} %bitcast.101), calls=%async_computation | async-start | bytes 4194304 | tf_op jit(solution)/shard_map/all_to_all | solution.py:157
  437.2 4.3 copy-start.9
  452.4 187.9 %copy-start.7 = (s32[128,1]{0,1:T(1,128)S(1)}, s32[128,1]{0,1:T(1,128)}, u32[]{:S(2)}) copy-start(s32[128,1]{0,1:T(1,128)} %param.24) | copy-start | bytes 1540
  452.4 188.0 %all-to-all-start.1 = ((bf16[32,16,2048]{2,1,0:T(8,128)(2,1)}), bf16[32,16,2048]{2,1,0:T(8,128)(2,1)}, u32[]{:S(2)}, u32[]{:S(2)}) async-start(bf16[32,16,2048]{2,1,0:T(8,128)(2,1)} %convolution_convert_fusion), calls=%async_computation.1 | async-start | bytes 4194304 | tf_op jit(solution)/shard_map/all_to_all | solution.py:162
  640.3 6.2 copy-start.8
Sparse Core Ops, SparseCore 0:
  15.2 187.0 all-gather.3
